TPU v7x, 32 devices: a whole 2x2x4 slice. The times are simulated.
32 devices in a mesh: layer: 2 (over x), row: 4 (over z), col: 4 (over y, core).
Axes of the slice: x: 2, y: 2, z: 4, core: 2. Of those that a mesh axis runs over, the one named last changes fastest.
Arguments:
- covariance: float32 [16384, 8192], P(('layer', 'row'), 'col'), parts along dimension 0, may hold values from -2 to 20, as said below
- weight: bfloat16 [16384, 2, 1024], P(('layer', 'col', 'row')), parts along dimension 0, may hold values from -6 to 6
- factor_a: bfloat16 [16384, 2, 256], P(('layer', 'col', 'row')), parts along dimension 0, may hold values from -1.5 to 1.5
- factor_b: bfloat16 [4, 256, 1024], P('layer', ('row', 'col')), parts along dimension 0, may hold values from -1.5 to 1.5
Outputs:
- new_a: float32 [16384, 2, 256], P(('layer', 'col', 'row')), parts along dimension 0
- new_b: float32 [4, 256, 1024], P('layer', ('row', 'col')), parts along dimension 0
There are 2 independent parts, one for each index of `layer`. A program takes and returns all parts, laid end to end along the dimension named above; each array names one. Nothing has to cross between parts.
Inputs may be any that keep to these rules, and one draw needn't show every extreme that they name: covariance is symmetric and positive definite.
All inputs are finite; a program needn't handle non-finite values.
Results may differ from a plain program's by a relative error of at most 0.0012.
Values may be sent and summed in bfloat16 or wider, within the bound.
No kernel may reach another device: no remote copies, remote signals or barrier semaphores. Data moves between devices by JAX's collectives and lax.ppermute only.
A program may use at most 64 MiB of HBM per device.

v0:
```python
import jax
import jax.numpy as jnp
from jax import lax
from jax.sharding import PartitionSpec as P

D = 8192
O = 1024
R = 256


def reorder_slots(spread):
    side = lax.axis_size("row")
    total = side * side
    return spread.reshape(side, side, -1).transpose(1, 0, 2).reshape(total, -1)


def transpose_full(values):
    side = lax.axis_size("row")
    flat = values.reshape(side * side, -1)
    spread = lax.all_to_all(flat, ("row", "col"), split_axis=0, concat_axis=0, tiled=True)
    landed = lax.all_to_all(
        reorder_slots(spread), ("row", "col"), split_axis=0, concat_axis=0, tiled=True
    )
    return landed.reshape(values.shape)


def per_device(covariance, weight, factor_a, factor_b):
    highest = lax.Precision.HIGHEST
    row_count = weight.shape[0]
    full_b = lax.all_gather(factor_b, ("row", "col"), axis=1, tiled=True)
    right_f = full_b.astype(jnp.float32)
    diff_one = (
        weight.astype(jnp.float32)
        - jnp.einsum("nkr,kro->nko", factor_a, full_b, preferred_element_type=jnp.float32)
    ).astype(jnp.bfloat16)
    panels = lax.all_gather(
        jnp.einsum("nko,kro->nkr", diff_one, full_b, preferred_element_type=jnp.float32),
        "row",
        axis=0,
        tiled=True,
    )
    panel_flat = panels.reshape(panels.shape[0], -1)
    cov_rows = covariance
    grad_one = lax.psum_scatter(
        jnp.dot(cov_rows, panel_flat, precision=highest, preferred_element_type=jnp.float32),
        "col",
        scatter_dimension=0,
        tiled=True,
    )
    grad_one = transpose_full(grad_one)
    new_a = factor_a.astype(jnp.float32) + 4.0 / O * grad_one.reshape(row_count, 2, R)
    diff_two = (
        weight.astype(jnp.float32) - jnp.einsum("nkr,kro->nko", new_a, right_f, precision=highest)
    ).astype(jnp.bfloat16)
    a_panel = lax.all_gather(new_a.reshape(row_count, 2 * R), "row", axis=0, tiled=True)
    cov_rows = covariance
    field = lax.psum_scatter(
        jnp.dot(cov_rows, a_panel, precision=highest, preferred_element_type=jnp.float32),
        "col",
        scatter_dimension=0,
        tiled=True,
    )
    field = transpose_full(field)
    partial_value = jnp.einsum(
        "nkr,nko->kro",
        field.reshape(row_count, 2, R),
        diff_two.astype(jnp.float32),
        precision=highest,
    )
    summed = lax.psum(partial_value, ("row", "col"))
    share_rows = factor_b.shape[1]
    linear_id = lax.axis_index("row") * lax.axis_size("col") + lax.axis_index("col")
    own_share = lax.dynamic_slice_in_dim(summed, linear_id * share_rows, share_rows, 1)
    new_b = factor_b.astype(jnp.float32) + 8.0 / D * own_share
    return (new_a, new_b)


def solution(mesh):
    in_specs = (
        P(("layer", "row"), "col"),
        P(("layer", "col", "row"), None, None),
        P(("layer", "col", "row"), None, None),
        P("layer", ("row", "col"), None),
    )
    out_specs = (P(("layer", "col", "row"), None, None), P("layer", ("row", "col"), None))
    return jax.shard_map(
        per_device, mesh=mesh, in_specs=in_specs, out_specs=out_specs, check_vma=False
    )
```

profile of v0, /device:TPU:0, one launch (start us, length us, event | category | flops | bytes accessed | tf_op | source)
XLA Modules:
  0.0 676.0 jit_solution(4953905984134823521)
XLA Ops:
  8.0 4.7 copy.27
  12.7 38.1 %all-gather.4.cloned.1.call-done = bf16[2,256,1024]{2,1,0:T(8,128)(2,1)} async-done(((bf16[2,16,1024]{2,1,0:T(8,128)(2,1)}), bf16[2,256,1024]{2,1,0:T(8,128)(2,1)}) %all-gather.4.cloned.1.call-update) | async-done | bytes 1048592 | tf_op jit(solution)/shard_map/all_gather | solution.py:30
  50.8 4.3 fusion.3
  55.2 79.8 %all-gather.6.cloned.1.call-done = f32[2048,2,256]{2,0,1:T(8,128)} async-done(((f32[512,2,256]{2,0,1:T(8,128)}), f32[2048,2,256]{2,0,1:T(8,128)}) %all-gather.6.cloned.1.call-update) | async-done | bytes 4194320 | tf_op jit(solution)/shard_map/all_gather | solution.py:36
  135.0 5.4 copy.30
  140.4 32.4 %convolution_bitcast_fusion.1 = f32[2048,512]{0,1:T(8,128)} fusion(f32[2048,512]{0,1:T(8,128)} %bitcast.35, f32[2048,2048]{1,0:T(8,128)} %param.4), kind=kOutput, calls=%fused_computation.5 | convolution fusion | flops 25769803776 | bytes 25165824 | tf_op jit(solution)/shard_map/dot_general | solution.py:45
  172.8 43.0 %reduce-scatter.3.cloned.1.call-done = f32[512,512]{0,1:T(8,128)} async-done(((f32[2048,512]{0,1:T(8,128)}), f32[512,512]{0,1:T(8,128)}) %reduce-scatter.3.cloned.1.call-update) | async-done | bytes 1048592 | tf_op jit(solution)/shard_map/reduce_scatter | solution.py:44
  217.4 2.2 all_to_all.32
  219.6 29.9 %all_to_all.40 = f32[16,1,16384]{2,1,0:T(1,128)S(1)} all-to-all(f32[16,1,16384]{2,1,0:T(1,128)} %all_to_all.32), channel_id=1, replica_groups=mesh['layer'=2,'row'=4,'col'=4] {'row','col'}, dimensions={0} | all-to-all | bytes 2097152 | tf_op jit(solution)/shard_map/all_to_all | solution.py:20
  249.5 3.7 reduce
  254.8 1.6 copy.33
  256.5 2.6 all_to_all.33
  259.1 29.5 %all_to_all.41 = f32[16,1,16384]{2,1,0:T(1,128)S(1)} all-to-all(f32[16,1,16384]{2,1,0:T(1,128)S(1)} %all_to_all.33), channel_id=1, replica_groups=mesh['layer'=2,'row'=4,'col'=4] {'row','col'}, dimensions={0} | all-to-all | bytes 2097152 | tf_op jit(solution)/shard_map/all_to_all | solution.py:21
  288.6 3.0 multiply_reduce_fusion
  291.6 1.9 mul.23
  296.1 81.2 %all-gather.8.cloned.1.call-done = f32[2048,512]{1,0:T(8,128)} async-done(((f32[512,512]{1,0:T(8,128)}), f32[2048,512]{1,0:T(8,128)}) %all-gather.8.cloned.1.call-update) | async-done | bytes 4194320 | tf_op jit(solution)/shard_map/all_gather | solution.py:55
  377.3 57.6 %convolution_bitcast_fusion = f32[2048,512]{0,1:T(8,128)} fusion(f32[2048,512]{1,0:T(8,128)} %all-gather.8.cloned.1.call-done, f32[2048,2048]{1,0:T(8,128)} %param.4), kind=kOutput, calls=%fused_computation.4 | convolution fusion | flops 25769803776 | bytes 25165824 | tf_op jit(solution)/shard_map/dot_general | solution.py:58
  435.0 43.1 %reduce-scatter.5.cloned.1.call-done = f32[512,512]{0,1:T(8,128)} async-done(((f32[2048,512]{0,1:T(8,128)}), f32[512,512]{0,1:T(8,128)}) %reduce-scatter.5.cloned.1.call-update) | async-done | bytes 1048592 | tf_op jit(solution)/shard_map/reduce_scatter | solution.py:57
  478.0 2.6 copy.35
  480.6 3.4 all_to_all.34
  484.0 29.5 %all_to_all.42 = f32[16,1,16384]{2,1,0:T(1,128)} all-to-all(f32[16,1,16384]{2,1,0:T(1,128)} %all_to_all.34), channel_id=1, replica_groups=mesh['layer'=2,'row'=4,'col'=4] {'row','col'}, dimensions={0} | all-to-all | bytes 2097152 | tf_op jit(solution)/shard_map/all_to_all | solution.py:20
  513.5 4.7 reduce.2
  518.3 2.5 reshape.41
  520.8 2.9 copy.57
  523.7 3.3 all_to_all.35
  527.0 5.1 all-to-all-start.3
  532.4 4.5 fusion.1
  536.9 18.1 %all-to-all-done.3 = f32[16,1,16384]{2,1,0:T(1,128)} async-done(((f32[16,1,16384]{2,1,0:T(1,128)}), f32[16,1,16384]{2,1,0:T(1,128)}, u32[]{:S(2)}, u32[]{:S(2)}) %all-to-all-start.3) | async-done | bytes 1048608 | tf_op jit(solution)/shard_map/all_to_all | solution.py:21
  555.0 4.7 reduce.3
  559.8 2.1 reshape_reshape.4
  561.9 4.8 fusion.4
  566.7 100.4 %all-reduce.2.cloned.1.call-done = f32[2,256,1024]{2,1,0:T(8,128)} async-done(((f32[2,256,1024]{2,1,0:T(8,128)}), f32[2,256,1024]{2,1,0:T(8,128)}) %all-reduce.2.cloned.1.call-update) | async-done | bytes 2097168 | tf_op jit(solution)/shard_map/psum | solution.py:70
  (25 shorter events, 8.5 us)
Async XLA Ops:
  7.2 43.6 %copy-start.2 = (bf16[512,2,256]{2,1,0:T(2,128)(2,1)S(1)}, bf16[512,2,256]{2,1,0:T(2,128)(2,1)}, u32[]{:S(2)}) copy-start(bf16[512,2,256]{2,1,0:T(2,128)(2,1)} %param.6) | copy-start | bytes 1572868
  7.2 43.6 %all-gather.4.cloned.1.call-start = ((), (), s32[]{:S(2)}) async-start(), calls=%async_computation.6 | async-start | bytes 1114112 | tf_op jit(solution)/shard_map/all_gather | solution.py:30
  7.9 127.1 %all-gather.6.cloned.1.call-start = ((), (), s32[]{:S(2)}) async-start(), calls=%async_computation.7 | async-start | bytes 5242880 | tf_op jit(solution)/shard_map/all_gather | solution.py:36
  55.2 160.7 %reduce-scatter.3.cloned.1.call-start = ((), (), s32[]{:S(2)}) async-start(), calls=%async_computation.8 | async-start | bytes 5242880 | tf_op jit(solution)/shard_map/reduce_scatter | solution.py:44
  172.8 204.5 %all-gather.8.cloned.1.call-start = ((), (), s32[]{:S(2)}) async-start(), calls=%async_computation.9 | async-start | bytes 5242880 | tf_op jit(solution)/shard_map/all_gather | solution.py:55
  294.9 237.5 %copy-start = (f32[128,8,256]{2,1,0:T(8,128)}, f32[128,8,256]{2,1,0:T(8,128)S(1)}, u32[]{:S(2)}) copy-start(f32[128,8,256]{2,1,0:T(8,128)S(1)} %convert_add_fusion) | copy-start | bytes 3145732
  296.1 181.9 %reduce-scatter.5.cloned.1.call-start = ((), (), s32[]{:S(2)}) async-start(), calls=%async_computation.10 | async-start | bytes 5242880 | tf_op jit(solution)/shard_map/reduce_scatter | solution.py:57
  527.0 28.0 %all-to-all-start.3 = ((f32[16,1,16384]{2,1,0:T(1,128)}), f32[16,1,16384]{2,1,0:T(1,128)}, u32[]{:S(2)}, u32[]{:S(2)}) async-start(f32[16,1,16384]{2,1,0:T(1,128)} %all_to_all.35), calls=%async_computation.5 | async-start | bytes 2097152 | tf_op jit(solution)/shard_map/all_to_all | solution.py:21
  532.1 135.0 %all-reduce.2.cloned.1.call-start = ((), (), s32[]{:S(2)}) async-start(), calls=%async_computation.11 | async-start | bytes 4194304 | tf_op jit(solution)/shard_map/psum | solution.py:70
  536.9 24.9 %copy-start.1 = (bf16[512,2,1024]{0,2,1:T(8,128)(2,1)S(1)}, bf16[512,2,1024]{0,2,1:T(8,128)(2,1)}, u32[]{:S(2)}) copy-start(bf16[512,2,1024]{0,2,1:T(8,128)(2,1)} %fusion.1) | copy-start | bytes 6291460
  561.9 105.2 %copy-start.3 = (bf16[2,16,1024]{2,1,0:T(8,128)(2,1)S(1)}, bf16[2,16,1024]{2,1,0:T(8,128)(2,1)}, u32[]{:S(2)}) copy-start(bf16[2,16,1024]{2,1,0:T(8,128)(2,1)} %param.7) | copy-start | bytes 196612
Sparse Core Ops, SparseCore 0:
  10.2 40.5 all-gather.3
  55.3 79.7 all-gather.5
  172.9 42.9 reduce-scatter.2
  296.2 81.0 all-gather.7
  435.1 42.9 reduce-scatter.4
  566.8 100.2 all-reduce.1
where the time goes:
time: 683 us; the launch traced here: 676 us
  waiting for transfers between devices  404 us (59%)
  matrix products  104 us (15%)
  blocking collectives  88.9 us (13%)
  local copies, waits for them, and re-layouts  39.6 us (6%)
  other arithmetic  19.2 us (3%)
  between operations  14.7 us (2%)
    psum x1, waiting for transfers between devices, per_device(): summed = lax.psum(partial_value, ('row', 'col'))  100 us
    all_gather x1, waiting for transfers between devices, per_device(): lax.all_gather(new_a.reshape(row_count, 2 * R), 'row', axis=0, tiled=True)  81.2 us
    all_gather x1, waiting for transfers between devices, per_device(): lax.all_gather(jnp.einsum('nko,kro->nkr', diff_one, full_b, preferred_ele...  79.8 us
    all_to_all x2, blocking collectives, transpose_full(): lax.all_to_all(flat, ('row', 'col'), split_axis=0, concat_axis=0, tiled=T...  59.4 us
    dot_general x1, matrix products, per_device(): jnp.dot(cov_rows, a_panel, precision=highest, preferred_element_type=jnp....  57.6 us
    reduce_scatter x1, waiting for transfers between devices, per_device(): lax.psum_scatter(jnp.dot(cov_rows, a_panel, precision=highest, preferred_...  43.1 us
    reduce_scatter x1, waiting for transfers between devices, per_device(): lax.psum_scatter(jnp.dot(cov_rows, panel_flat, precision=highest, preferr...  43 us
    all_gather x1, waiting for transfers between devices, per_device(): full_b = lax.all_gather(factor_b, ('row', 'col'), axis=1, tiled=True)  38.1 us
  transfers between devices with their start and end apart: 7, of which 7 were waited for; matrix products, arithmetic and copies ran while one was open for 1% of the time, Pallas kernels for 0%

commit v1 on v0

--- a/solution.py
+++ b/solution.py
@@ -67,7 +67,7 @@
         diff_two.astype(jnp.float32),
         precision=highest,
     )
-    summed = lax.psum(partial_value, ("row", "col"))
+    summed = lax.psum(lax.psum(partial_value, "row"), "col")
     share_rows = factor_b.shape[1]
     linear_id = lax.axis_index("row") * lax.axis_size("col") + lax.axis_index("col")
     own_share = lax.dynamic_slice_in_dim(summed, linear_id * share_rows, share_rows, 1)

time: 683 us -> 724 us (1.060)
  waiting for transfers between devices: 404 us -> 445 us
    psum x1 -> x2, waiting for transfers between devices: 100 us -> 141 us  [per_device(): summed = lax.psum(lax.psum(partial_value, 'row'), 'col')]
  transfers between devices with their start and end apart: 7 -> 8, of which waited for: 7 -> 8; matrix products, arithmetic and copies ran while one was open for 1% -> 1% of each run, Pallas kernels for 0% -> 0%
where the time goes in v1:
time: 724 us; the launch traced here: 717 us
  waiting for transfers between devices  445 us (61%)
  matrix products  104 us (14%)
  blocking collectives  88.9 us (12%)
  local copies, waits for them, and re-layouts  39.6 us (5%)
  other arithmetic  19.2 us (3%)
  between operations  14.7 us (2%)
    psum x2, waiting for transfers between devices, per_device(): summed = lax.psum(lax.psum(partial_value, 'row'), 'col')  141 us
    all_gather x1, waiting for transfers between devices, per_device(): lax.all_gather(new_a.reshape(row_count, 2 * R), 'row', axis=0, tiled=True)  81.2 us
    all_gather x1, waiting for transfers between devices, per_device(): lax.all_gather(jnp.einsum('nko,kro->nkr', diff_one, full_b, preferred_ele...  79.8 us
    all_to_all x2, blocking collectives, transpose_full(): lax.all_to_all(flat, ('row', 'col'), split_axis=0, concat_axis=0, tiled=T...  59.4 us
    dot_general x1, matrix products, per_device(): jnp.dot(cov_rows, a_panel, precision=highest, preferred_element_type=jnp....  57.6 us
    reduce_scatter x1, waiting for transfers between devices, per_device(): lax.psum_scatter(jnp.dot(cov_rows, a_panel, precision=highest, preferred_...  43.1 us
    reduce_scatter x1, waiting for transfers between devices, per_device(): lax.psum_scatter(jnp.dot(cov_rows, panel_flat, precision=highest, preferr...  43 us
    all_gather x1, waiting for transfers between devices, per_device(): full_b = lax.all_gather(factor_b, ('row', 'col'), axis=1, tiled=True)  38.1 us
  transfers between devices with their start and end apart: 8, of which 8 were waited for; matrix products, arithmetic and copies ran while one was open for 1% of the time, Pallas kernels for 0%

profile of v1, /device:TPU:0, one launch (start us, length us, event | category | flops | bytes accessed | tf_op | source)
XLA Modules:
  0.0 716.8 jit_solution(7906713931103597626)
XLA Ops:
  8.0 4.7 copy.27
  12.7 38.1 %all-gather.4.cloned.1.call-done = bf16[2,256,1024]{2,1,0:T(8,128)(2,1)} async-done(((bf16[2,16,1024]{2,1,0:T(8,128)(2,1)}), bf16[2,256,1024]{2,1,0:T(8,128)(2,1)}) %all-gather.4.cloned.1.call-update) | async-done | bytes 1048592 | tf_op jit(solution)/shard_map/all_gather | solution.py:30
  50.8 4.3 fusion.3
  55.2 79.8 %all-gather.6.cloned.1.call-done = f32[2048,2,256]{2,0,1:T(8,128)} async-done(((f32[512,2,256]{2,0,1:T(8,128)}), f32[2048,2,256]{2,0,1:T(8,128)}) %all-gather.6.cloned.1.call-update) | async-done | bytes 4194320 | tf_op jit(solution)/shard_map/all_gather | solution.py:36
  135.0 5.4 copy.30
  140.4 32.4 %convolution_bitcast_fusion.1 = f32[2048,512]{0,1:T(8,128)} fusion(f32[2048,512]{0,1:T(8,128)} %bitcast.35, f32[2048,2048]{1,0:T(8,128)} %param.4), kind=kOutput, calls=%fused_computation.5 | convolution fusion | flops 25769803776 | bytes 25165824 | tf_op jit(solution)/shard_map/dot_general | solution.py:45
  172.8 43.0 %reduce-scatter.3.cloned.1.call-done = f32[512,512]{0,1:T(8,128)} async-done(((f32[2048,512]{0,1:T(8,128)}), f32[512,512]{0,1:T(8,128)}) %reduce-scatter.3.cloned.1.call-update) | async-done | bytes 1048592 | tf_op jit(solution)/shard_map/reduce_scatter | solution.py:44
  217.4 2.2 all_to_all.32
  219.6 29.9 %all_to_all.40 = f32[16,1,16384]{2,1,0:T(1,128)S(1)} all-to-all(f32[16,1,16384]{2,1,0:T(1,128)} %all_to_all.32), channel_id=1, replica_groups=mesh['layer'=2,'row'=4,'col'=4] {'row','col'}, dimensions={0} | all-to-all | bytes 2097152 | tf_op jit(solution)/shard_map/all_to_all | solution.py:20
  249.5 3.7 reduce
  256.5 2.6 all_to_all.33
  259.1 29.5 %all_to_all.41 = f32[16,1,16384]{2,1,0:T(1,128)S(1)} all-to-all(f32[16,1,16384]{2,1,0:T(1,128)S(1)} %all_to_all.33), channel_id=1, replica_groups=mesh['layer'=2,'row'=4,'col'=4] {'row','col'}, dimensions={0} | all-to-all | bytes 2097152 | tf_op jit(solution)/shard_map/all_to_all | solution.py:21
  288.6 3.0 multiply_reduce_fusion
  291.6 1.9 mul.23
  296.1 81.2 %all-gather.8.cloned.1.call-done = f32[2048,512]{1,0:T(8,128)} async-done(((f32[512,512]{1,0:T(8,128)}), f32[2048,512]{1,0:T(8,128)}) %all-gather.8.cloned.1.call-update) | async-done | bytes 4194320 | tf_op jit(solution)/shard_map/all_gather | solution.py:55
  377.3 57.6 %convolution_bitcast_fusion = f32[2048,512]{0,1:T(8,128)} fusion(f32[2048,512]{1,0:T(8,128)} %all-gather.8.cloned.1.call-done, f32[2048,2048]{1,0:T(8,128)} %param.4), kind=kOutput, calls=%fused_computation.4 | convolution fusion | flops 25769803776 | bytes 25165824 | tf_op jit(solution)/shard_map/dot_general | solution.py:58
  435.0 43.1 %reduce-scatter.5.cloned.1.call-done = f32[512,512]{0,1:T(8,128)} async-done(((f32[2048,512]{0,1:T(8,128)}), f32[512,512]{0,1:T(8,128)}) %reduce-scatter.5.cloned.1.call-update) | async-done | bytes 1048592 | tf_op jit(solution)/shard_map/reduce_scatter | solution.py:57
  478.0 2.6 copy.35
  480.6 3.4 all_to_all.34
  484.0 29.5 %all_to_all.42 = f32[16,1,16384]{2,1,0:T(1,128)} all-to-all(f32[16,1,16384]{2,1,0:T(1,128)} %all_to_all.34), channel_id=1, replica_groups=mesh['layer'=2,'row'=4,'col'=4] {'row','col'}, dimensions={0} | all-to-all | bytes 2097152 | tf_op jit(solution)/shard_map/all_to_all | solution.py:20
  513.5 4.7 reduce.2
  518.3 2.5 reshape.41
  520.8 2.9 copy.57
  523.7 3.3 all_to_all.35
  527.0 5.1 all-to-all-start.3
  532.4 4.5 fusion.1
  536.9 18.1 %all-to-all-done.3 = f32[16,1,16384]{2,1,0:T(1,128)} async-done(((f32[16,1,16384]{2,1,0:T(1,128)}), f32[16,1,16384]{2,1,0:T(1,128)}, u32[]{:S(2)}, u32[]{:S(2)}) %all-to-all-start.3) | async-done | bytes 1048608 | tf_op jit(solution)/shard_map/all_to_all | solution.py:21
  555.0 4.7 reduce.3
  559.8 2.1 reshape_reshape.4
  561.9 4.8 fusion.4
  566.8 88.4 %all-reduce.3.cloned.1.call-done = f32[2,256,1024]{2,1,0:T(8,128)} async-done(((f32[2,256,1024]{2,1,0:T(8,128)}), f32[2,256,1024]{2,1,0:T(8,128)}) %all-reduce.3.cloned.1.call-update) | async-done | bytes 2097168 | tf_op jit(solution)/shard_map/psum | solution.py:70
  655.2 52.8 %all-reduce.5.cloned.1.call-done = f32[2,256,1024]{2,1,0:T(8,128)} async-done(((f32[2,256,1024]{2,1,0:T(8,128)}), f32[2,256,1024]{2,1,0:T(8,128)}) %all-reduce.5.cloned.1.call-update) | async-done | bytes 2097168 | tf_op jit(solution)/shard_map/psum | solution.py:70
  (28 shorter events, 10.2 us)
Async XLA Ops:
  7.2 43.6 %copy-start.2 = (bf16[512,2,256]{2,1,0:T(2,128)(2,1)S(1)}, bf16[512,2,256]{2,1,0:T(2,128)(2,1)}, u32[]{:S(2)}) copy-start(bf16[512,2,256]{2,1,0:T(2,128)(2,1)} %param.6) | copy-start | bytes 1572868
  7.2 43.6 %all-gather.4.cloned.1.call-start = ((), (), s32[]{:S(2)}) async-start(), calls=%async_computation.6 | async-start | bytes 1114112 | tf_op jit(solution)/shard_map/all_gather | solution.py:30
  7.9 127.1 %all-gather.6.cloned.1.call-start = ((), (), s32[]{:S(2)}) async-start(), calls=%async_computation.7 | async-start | bytes 5242880 | tf_op jit(solution)/shard_map/all_gather | solution.py:36
  55.2 160.7 %reduce-scatter.3.cloned.1.call-start = ((), (), s32[]{:S(2)}) async-start(), calls=%async_computation.8 | async-start | bytes 5242880 | tf_op jit(solution)/shard_map/reduce_scatter | solution.py:44
  172.8 204.5 %all-gather.8.cloned.1.call-start = ((), (), s32[]{:S(2)}) async-start(), calls=%async_computation.9 | async-start | bytes 5242880 | tf_op jit(solution)/shard_map/all_gather | solution.py:55
  294.9 237.5 %copy-start = (f32[128,8,256]{2,1,0:T(8,128)}, f32[128,8,256]{2,1,0:T(8,128)S(1)}, u32[]{:S(2)}) copy-start(f32[128,8,256]{2,1,0:T(8,128)S(1)} %convert_add_fusion) | copy-start | bytes 3145732
  296.1 181.9 %reduce-scatter.5.cloned.1.call-start = ((), (), s32[]{:S(2)}) async-start(), calls=%async_computation.10 | async-start | bytes 5242880 | tf_op jit(solution)/shard_map/reduce_scatter | solution.py:57
  527.0 28.0 %all-to-all-start.3 = ((f32[16,1,16384]{2,1,0:T(1,128)}), f32[16,1,16384]{2,1,0:T(1,128)}, u32[]{:S(2)}, u32[]{:S(2)}) async-start(f32[16,1,16384]{2,1,0:T(1,128)} %all_to_all.35), calls=%async_computation.5 | async-start | bytes 2097152 | tf_op jit(solution)/shard_map/all_to_all | solution.py:21
  532.1 123.0 %all-reduce.3.cloned.1.call-start = ((), (), s32[]{:S(2)}) async-start(), calls=%async_computation.11 | async-start | bytes 4194304 | tf_op jit(solution)/shard_map/psum | solution.py:70
  536.9 24.9 %copy-start.1 = (bf16[512,2,1024]{0,2,1:T(8,128)(2,1)S(1)}, bf16[512,2,1024]{0,2,1:T(8,128)(2,1)}, u32[]{:S(2)}) copy-start(bf16[512,2,1024]{0,2,1:T(8,128)(2,1)} %fusion.1) | copy-start | bytes 6291460
  561.9 146.1 %copy-start.3 = (bf16[2,16,1024]{2,1,0:T(8,128)(2,1)S(1)}, bf16[2,16,1024]{2,1,0:T(8,128)(2,1)}, u32[]{:S(2)}) copy-start(bf16[2,16,1024]{2,1,0:T(8,128)(2,1)} %param.7) | copy-start | bytes 196612
  566.7 141.2 %all-reduce.5.cloned.1.call-start = ((), (), s32[]{:S(2)}) async-start(), calls=%async_computation.12 | async-start | bytes 4194304 | tf_op jit(solution)/shard_map/psum | solution.py:70
Sparse Core Ops, SparseCore 0:
  10.2 40.5 all-gather.3
  55.3 79.7 all-gather.5
  172.9 42.9 reduce-scatter.2
  296.2 81.0 all-gather.7
  435.1 42.9 reduce-scatter.4
  566.8 88.2 all-reduce.2
  657.5 50.4 all-reduce.4
